TPU v7x, 512 devices: a whole 4x8x8 slice. The times are simulated.
512 devices in a mesh: section: 16 (over z_lo, y), shard: 32 (over x, z_hi, core).
Axes of the slice: x: 4, y: 8, z: 8 (z_hi: 4, z_lo: 2; z = z_hi * 2 + z_lo), core: 2. Of those that a mesh axis runs over, the one named last changes fastest.
Arguments:
- layer_input: bfloat16 [16, 4096, 3072], P('section', 'shard'), may hold values from -150 to 150
- out_grad: bfloat16 [16, 4096, 3072], P('section', 'shard'), may hold values from -60 to 60
- modulation: float32 [16, 4, 3, 3072], P('section'), may hold values from -3 to 3
- proj_weight: bfloat16 [16, 3072, 3072], P('section', 'shard'), may hold values from -0.109375 to 0.109375
Outputs:
- handoff: bfloat16 [16, 4096, 3072], P('section', 'shard')
- mod_grad: float32 [16, 4, 3, 3072], P('section')
All inputs are finite; a program needn't handle non-finite values.
Results may differ from a plain program's by a relative error of at most 0.0029.
Values may be sent and summed in bfloat16 or wider, within the bound.
A program may use at most 128 MiB of HBM per device.

v0:
```python
import jax
import jax.numpy as jnp
from jax import lax
from jax.sharding import PartitionSpec as P

SEQS = 4


def swapped(value, axis, apart):
    mask = 2**apart
    pairs = [(source, source ^ mask) for source in range(lax.axis_size(axis))]
    return lax.ppermute(value, axis, pairs)


def passed_along(value, axis, steps):
    count = lax.axis_size(axis)
    leading, last = (max(0, -steps), min(count, count - steps))
    return lax.ppermute(value, axis, [(source, source + steps) for source in range(leading, last)])


def select_rows(token_ids, seq_length):
    sample = token_ids // seq_length
    return (sample[:, None] == jnp.arange(SEQS, dtype=jnp.int32)[None, :]).astype(jnp.float32)


def norm_rows(activation):
    values = activation.astype(jnp.float32)
    center = values - jnp.mean(values, axis=-1, keepdims=True)
    variance = jnp.mean(center * center, axis=-1, keepdims=True)
    inv_scale = lax.rsqrt(variance + 1e-06)
    return (center * inv_scale, inv_scale)


def on_device(layer_input, out_grad, modulation, proj_weight):
    shard_count = lax.axis_size("shard")
    my_index = lax.axis_index("shard")
    group_bits = 1
    group_size = 2**group_bits
    own_input = layer_input[0]
    own_grad = out_grad[0]
    mod_table = modulation[0]
    weight_rows = proj_weight[0]
    row_count, feat_count = own_input.shape
    col_count = feat_count // group_size
    seq_length = row_count * shard_count // SEQS
    position = my_index % group_size
    own_sample = my_index * row_count // seq_length
    own_mod = lax.dynamic_index_in_dim(mod_table, own_sample, 0, keepdims=False)
    sample_hot = (jnp.arange(SEQS, dtype=jnp.int32) == own_sample).astype(jnp.float32)
    normed, inv_scale = norm_rows(own_input)
    modulated = (normed * (1.0 + own_mod[1]) + own_mod[0]).astype(jnp.bfloat16)
    joined = jnp.stack([modulated, own_grad], axis=0)
    bit_number = 0
    partner = swapped(joined, "shard", bit_number)
    upper_side = my_index // 2**bit_number % 2 == 1
    lower_part = jnp.where(upper_side, partner, joined)
    upper_part = jnp.where(upper_side, joined, partner)
    joined = jnp.concatenate([lower_part, upper_part], axis=1)
    group_input = joined[0]
    group_grad = joined[1]
    piece_rows = weight_rows.shape[0]
    pieces = jnp.transpose(weight_rows.reshape(piece_rows, group_size, col_count), (1, 0, 2))
    outgoing = jnp.broadcast_to(
        pieces[None], (shard_count // group_size, group_size, piece_rows, col_count)
    )
    outgoing = outgoing.reshape(shard_count, piece_rows, col_count)
    incoming = lax.all_to_all(outgoing, "shard", split_axis=0, concat_axis=0, tiled=True)
    weight_cols = incoming.reshape(feat_count, col_count)
    group_ids = (my_index - position) * row_count + jnp.arange(
        group_size * row_count, dtype=jnp.int32
    )
    group_select = select_rows(group_ids, seq_length)
    col_start = position * col_count
    gate_table = lax.dynamic_slice_in_dim(mod_table[:, 2], col_start, col_count, 1)
    gate_cols = jnp.dot(group_select, gate_table, precision=lax.Precision.HIGHEST)
    grad_cols = lax.dynamic_slice_in_dim(group_grad, col_start, col_count, 1).astype(jnp.float32)
    branch = jnp.dot(group_input, weight_cols, preferred_element_type=jnp.float32)
    scaled_grad = (gate_cols * grad_cols).astype(jnp.bfloat16)
    partial_grad = lax.dot_general(
        scaled_grad, weight_cols, (((1,), (1,)), ((), ())), preferred_element_type=jnp.float32
    )
    gate_part = jnp.einsum(
        "rs,rd->sd", group_select, grad_cols * branch, precision=lax.Precision.HIGHEST
    )
    gate_full = lax.dynamic_update_slice(
        jnp.zeros((SEQS, feat_count), jnp.float32), gate_part, (jnp.int32(0), col_start)
    )
    current = partial_grad
    for bit_number in reversed(range(group_bits)):
        half_count = current.shape[0] // 2
        low_half = current[:half_count]
        high_half = current[half_count:]
        upper_side = my_index // 2**bit_number % 2 == 1
        kept_half = jnp.where(upper_side, high_half, low_half)
        sending = jnp.where(upper_side, low_half, high_half)
        current = kept_half + swapped(sending.astype(jnp.bfloat16), "shard", bit_number).astype(
            sending.dtype
        )
    grad_shift = sample_hot[:, None] * jnp.sum(current, axis=0)[None, :]
    grad_scale = sample_hot[:, None] * jnp.sum(current * normed, axis=0)[None, :]
    totals = lax.psum(jnp.stack([grad_shift, grad_scale, gate_full], axis=1), "shard")
    grad_norm = current * (1.0 + own_mod[1])
    centered = grad_norm - jnp.mean(grad_norm, axis=-1, keepdims=True)
    grad_in = own_grad.astype(jnp.float32) + inv_scale * (
        centered - normed * jnp.mean(grad_norm * normed, axis=-1, keepdims=True)
    )
    handoff = passed_along(grad_in.astype(jnp.bfloat16), "section", -1)
    return (handoff[None], totals[None])


def solution(mesh):
    in_specs = (
        P("section", "shard", None),
        P("section", "shard", None),
        P("section", None, None, None),
        P("section", "shard", None),
    )
    out_specs = (P("section", "shard", None), P("section", None, None, None))
    return jax.shard_map(
        on_device, mesh=mesh, in_specs=in_specs, out_specs=out_specs, check_vma=False
    )
```

profile of v0, /device:TPU:1, one launch (start us, length us, event | category | flops | bytes accessed | tf_op | source)
XLA Modules:
  0.0 538.5 jit_solution(8000382200679305160)
XLA Ops:
  7.2 2.2 reshape_squeeze.3
  9.4 4.7 broadcast_in_dim.8
  14.2 14.6 %all-to-all-start = ((bf16[32,96,1536]{2,1,0:T(8,128)(2,1)}), bf16[32,96,1536]{2,1,0:T(8,128)(2,1)}, u32[]{:S(2)}, u32[]{:S(2)}) async-start(bf16[32,96,1536]{2,1,0:T(8,128)(2,1)} %bitcast.61), calls=%async_computation | async-start | bytes 18874368 | tf_op jit(solution)/shard_map/all_to_all | solution.py:67
  30.1 1.3 pad_maximum_fusion.1
  31.4 2.2 collective-permute-start
  33.7 3.4 collective-permute-done
  37.0 1.6 broadcast_select_fusion.1
  39.0 0.8 copy-done.2
  39.8 0.5 copy-done.4
  40.3 1.2 copy-done.6
  41.5 1.8 fusion
  43.4 144.0 %all-to-all-done = bf16[32,96,1536]{2,1,0:T(8,128)(2,1)} async-done(((bf16[32,96,1536]{2,1,0:T(8,128)(2,1)}), bf16[32,96,1536]{2,1,0:T(8,128)(2,1)}, u32[]{:S(2)}, u32[]{:S(2)}) %all-to-all-start) | async-done | bytes 9437216 | tf_op jit(solution)/shard_map/all_to_all | solution.py:67
  187.4 5.6 %fusion.29 = f32[256,3072]{1,0:T(8,128)S(1)} fusion(bf16[256,1536]{1,0:T(8,128)(2,1)} %fusion, bf16[3072,1536]{1,0:T(8,128)(2,1)} %bitcast.9), kind=kOutput, calls=%fused_computation.59 | convolution fusion | flops 2415919104 | bytes 13369344 | tf_op jit(solution)/shard_map/dot_general | solution.py:79
  193.1 3.7 collective-permute-start.1
  196.9 5.2 convolution_multiply_fusion
  202.1 0.7 fusion.1
  202.8 1.0 fusion.13
  203.8 0.8 fusion.12
  204.5 1.3 collective-permute-start.2
  205.9 0.7 maximum_bitcast_fusion
  206.6 18.9 %collective-permute-done.2 = bf16[128,3072]{1,0:T(8,128)(2,1)S(1)} collective-permute-done((bf16[128,3072]{1,0:T(8,128)(2,1)S(1)}, bf16[128,3072]{1,0:T(8,128)(2,1)S(1)}, u32[]{:S(2)}, u32[]{:S(2)}) %collective-permute-start.2) | collective-permute-done | bytes 786464 | tf_op jit(solution)/shard_map/ppermute | solution.py:18
  225.5 304.5 %all-reduce.2.cloned.1.call-done = f32[1,4,3,3072]{3,1,2,0:T(4,128)} async-done(((f32[1,4,3,3072]{3,1,2,0:T(4,128)}), f32[1,4,3,3072]{3,1,2,0:T(4,128)}) %all-reduce.2.cloned.1.call-update) | async-done | bytes 147472 | tf_op jit(solution)/shard_map/psum | solution.py:101
  530.0 0.9 copy.10
  531.0 0.7 copy.11
  (36 shorter events, 2.1 us)
Async XLA Ops:
  14.2 14.7 %copy-start = (bf16[1,128,3072]{2,1,0:T(8,128)(2,1)S(1)}, bf16[1,128,3072]{2,1,0:T(8,128)(2,1)}, u32[]{:S(2)}) copy-start(bf16[1,128,3072]{2,1,0:T(8,128)(2,1)} %param.4) | copy-start | bytes 2359300
  14.2 173.2 %all-to-all-start = ((bf16[32,96,1536]{2,1,0:T(8,128)(2,1)}), bf16[32,96,1536]{2,1,0:T(8,128)(2,1)}, u32[]{:S(2)}, u32[]{:S(2)}) async-start(bf16[32,96,1536]{2,1,0:T(8,128)(2,1)} %bitcast.61), calls=%async_computation | async-start | bytes 18874368 | tf_op jit(solution)/shard_map/all_to_all | solution.py:67
  28.8 0.9 copy-start.9
  28.8 501.2 %all-reduce.2.cloned.1.call-start = ((), (), s32[]{:S(2)}) async-start(), calls=%async_computation.1 | async-start | bytes 294912 | tf_op jit(solution)/shard_map/psum | solution.py:101
  28.8 1.2 copy-start.1
  31.4 5.6 %collective-permute-start = (bf16[2,128,3072]{2,1,0:T(8,128)(2,1)}, bf16[2,128,3072]{2,1,0:T(8,128)(2,1)}, u32[]{:S(2)}, u32[]{:S(2)}) collective-permute-start(bf16[2,128,3072]{2,1,0:T(8,128)(2,1)} %pad_maximum_fusion.1), channel_id=1, source_target_pairs={{0,1},{1,0},{2,3},{3,2},{4,5},{5,4},{6,7},{7,6},{8,9},{9,8},{10,11... | collective-permute-start | bytes 4718600 | tf_op jit(solution)/shard_map/ppermute | solution.py:12
  38.7 1.2 copy-start.2
  38.7 1.7 copy-start.4
  40.3 1.2 copy-start.6
  187.3 9.5 %copy-start.5 = (bf16[2,128,3072]{2,1,0:T(8,128)(2,1)S(1)}, bf16[2,128,3072]{2,1,0:T(8,128)(2,1)}, u32[]{:S(2)}) copy-start(bf16[2,128,3072]{2,1,0:T(8,128)(2,1)} %copy-done.4) | copy-start | bytes 4718596
  187.3 9.5 %copy-start.7 = (bf16[1,256,3072]{2,1,0:T(8,128)(2,1)S(1)}, bf16[1,256,3072]{2,1,0:T(8,128)(2,1)}, u32[]{:S(2)}) copy-start(bf16[1,256,3072]{2,1,0:T(8,128)(2,1)} %copy-done.6) | copy-start | bytes 4718596
  192.9 3.9 copy-start.3
  193.1 9.7 %collective-permute-start.1 = (bf16[128,3072]{1,0:T(8,128)(2,1)S(1)}, bf16[128,3072]{1,0:T(8,128)(2,1)S(1)}, u32[]{:S(2)}, u32[]{:S(2)}) collective-permute-start(bf16[128,3072]{1,0:T(8,128)(2,1)S(1)} %select_convert_fusion), channel_id=1, source_target_pairs={{0,1},{1,0},{2,3},{3,2},{4,5},{5,4},{6,7},{7,6},{8,9},{9,8},{10,11... | collective-permute-start | bytes 2359304 | tf_op jit(solution)/shard_map/ppermute | solution.py:12
  204.5 21.0 %collective-permute-start.2 = (bf16[128,3072]{1,0:T(8,128)(2,1)S(1)}, bf16[128,3072]{1,0:T(8,128)(2,1)S(1)}, u32[]{:S(2)}, u32[]{:S(2)}) collective-permute-start(bf16[128,3072]{1,0:T(8,128)(2,1)S(1)} %fusion.12), channel_id=1, source_target_pairs={{32,0},{64,32},{96,64},{128,96},{160,128},{192,160},{224,192},{256... | collective-permute-start | bytes 2359304 | tf_op jit(solution)/shard_map/ppermute | solution.py:18
  530.0 1.0 copy-start.8
Sparse Core Ops, SparseCore 0:
  206.8 323.1 all-reduce.1
where the time goes:
time: 539 us
  waiting for transfers between devices  471 us (87%)
  starting transfers between devices  21.9 us (4%)
  between operations  14.3 us (3%)
  matrix products  13.3 us (2%)
  local copies, waits for them, and re-layouts  11.8 us (2%)
  other arithmetic  6.55 us (1%)
    psum x1, waiting for transfers between devices, on_device(): lax.psum(jnp.stack([grad_shift, grad_scale, gate_full], axis=1), 'shard')  304 us
    all_to_all x1, waiting for transfers between devices, on_device(): lax.all_to_all(outgoing, 'shard', split_axis=0, concat_axis=0, tiled=True)  144 us
    ppermute x1, waiting for transfers between devices, passed_along(): lax.ppermute(value, axis, [(source, source + steps) for source in range(l...  18.9 us
    all_to_all x1, starting transfers between devices, on_device(): lax.all_to_all(outgoing, 'shard', split_axis=0, concat_axis=0, tiled=True)  14.6 us
  transfers between devices with their start and end apart: 5, of which 4 were waited for; matrix products, arithmetic and copies ran while one was open for 2% of the time, Pallas kernels for 0%

commit v1 on v0

--- a/solution.py
+++ b/solution.py
@@ -98,7 +98,9 @@
         )
     grad_shift = sample_hot[:, None] * jnp.sum(current, axis=0)[None, :]
     grad_scale = sample_hot[:, None] * jnp.sum(current * normed, axis=0)[None, :]
-    totals = lax.psum(jnp.stack([grad_shift, grad_scale, gate_full], axis=1), "shard")
+    totals = jnp.sum(
+        lax.all_gather(jnp.stack([grad_shift, grad_scale, gate_full], axis=1), "shard"), axis=0
+    )
     grad_norm = current * (1.0 + own_mod[1])
     centered = grad_norm - jnp.mean(grad_norm, axis=-1, keepdims=True)
     grad_in = own_grad.astype(jnp.float32) + inv_scale * (

time: 539 us -> 345 us (0.64)
  waiting for transfers between devices: 471 us -> 272 us
    psum x1 -> x0, waiting for transfers between devices: 304 us -> none  [on_device(): lax.psum(jnp.stack([grad_shift, grad_scale, gate_full], axis=1), 'shard')]
    all_gather x0 -> x1, waiting for transfers between devices: none -> 105 us  [on_device(): lax.all_gather(jnp.stack([grad_shift, grad_scale, gate_full], axis=1), 's...]
  transfers between devices with their start and end apart: 5 -> 5, of which waited for: 4 -> 4; matrix products, arithmetic and copies ran while one was open for 2% -> 4% of each run, Pallas kernels for 0% -> 0%
where the time goes in v1:
time: 345 us; the launch traced here: 344 us
  waiting for transfers between devices  272 us (79%)
  starting transfers between devices  21.9 us (6%)
  between operations  14.3 us (4%)
  matrix products  13.3 us (4%)
  local copies, waits for them, and re-layouts  12.5 us (4%)
  other arithmetic  9.94 us (3%)
    all_to_all x1, waiting for transfers between devices, on_device(): lax.all_to_all(outgoing, 'shard', split_axis=0, concat_axis=0, tiled=True)  144 us
    all_gather x1, waiting for transfers between devices, on_device(): lax.all_gather(jnp.stack([grad_shift, grad_scale, gate_full], axis=1), 's...  105 us
    ppermute x1, waiting for transfers between devices, passed_along(): lax.ppermute(value, axis, [(source, source + steps) for source in range(l...  19.7 us
    all_to_all x1, starting transfers between devices, on_device(): lax.all_to_all(outgoing, 'shard', split_axis=0, concat_axis=0, tiled=True)  14.6 us
  transfers between devices with their start and end apart: 5, of which 4 were waited for; matrix products, arithmetic and copies ran while one was open for 4% of the time, Pallas kernels for 0%

profile of v1, /device:TPU:1, one launch (start us, length us, event | category | flops | bytes accessed | tf_op | source)
XLA Modules:
  0.0 344.3 jit_solution(9293381927958544892)
XLA Ops:
  7.2 2.2 reshape_squeeze.3
  9.4 4.7 %broadcast_in_dim.8 = bf16[16,2,96,1536]{3,2,1,0:T(8,128)(2,1)} broadcast(bf16[2,96,1536]{2,1,0:T(8,128)(2,1)S(1)} %copy.12), dimensions={1,2,3} | broadcast | bytes 10027008 | tf_op jit(solution)/shard_map/broadcast_in_dim | solution.py:63
  14.2 14.6 %all-to-all-start = ((bf16[32,96,1536]{2,1,0:T(8,128)(2,1)}), bf16[32,96,1536]{2,1,0:T(8,128)(2,1)}, u32[]{:S(2)}, u32[]{:S(2)}) async-start(bf16[32,96,1536]{2,1,0:T(8,128)(2,1)} %bitcast.61), calls=%async_computation | async-start | bytes 18874368 | tf_op jit(solution)/shard_map/all_to_all | solution.py:67
  30.1 1.3 pad_maximum_fusion.1
  31.4 2.2 collective-permute-start
  33.7 3.4 collective-permute-done
  37.0 1.6 broadcast_select_fusion.1
  39.0 0.8 copy-done.2
  40.3 1.2 copy-done.6
  41.5 1.8 fusion
  43.4 144.0 %all-to-all-done = bf16[32,96,1536]{2,1,0:T(8,128)(2,1)} async-done(((bf16[32,96,1536]{2,1,0:T(8,128)(2,1)}), bf16[32,96,1536]{2,1,0:T(8,128)(2,1)}, u32[]{:S(2)}, u32[]{:S(2)}) %all-to-all-start) | async-done | bytes 9437216 | tf_op jit(solution)/shard_map/all_to_all | solution.py:67
  187.4 5.6 %fusion.29 = f32[256,3072]{1,0:T(8,128)S(1)} fusion(bf16[256,1536]{1,0:T(8,128)(2,1)} %fusion, bf16[3072,1536]{1,0:T(8,128)(2,1)} %bitcast.9), kind=kOutput, calls=%fused_computation.59 | convolution fusion | flops 2415919104 | bytes 13369344 | tf_op jit(solution)/shard_map/dot_general | solution.py:79
  193.1 3.7 %collective-permute-start.1 = (bf16[128,3072]{1,0:T(8,128)(2,1)S(1)}, bf16[128,3072]{1,0:T(8,128)(2,1)S(1)}, u32[]{:S(2)}, u32[]{:S(2)}) collective-permute-start(bf16[128,3072]{1,0:T(8,128)(2,1)S(1)} %select_convert_fusion), channel_id=1, source_target_pairs={{0,1},{1,0},{2,3},{3,2},{4,5},{5,4},{6,7},{7,6},{8,9},{9,8},{10,11... | collective-permute-start | bytes 2359304 | tf_op jit(solution)/shard_map/ppermute | solution.py:12
  196.9 5.2 %convolution_multiply_fusion = f32[256,1536]{1,0:T(8,128)S(1)} fusion(bf16[3072,1536]{1,0:T(8,128)(2,1)} %bitcast.9, bf16[2,128,3072]{2,1,0:T(8,128)(2,1)S(1)} %copy-done.5, bf16[2,128,3072]{2,1,0:T(8,128)(2,1)S(1)} %copy-done.3, bf16[1,256,3072]{2,1,0:T(8,128)(2,1)S(1)} %get-tuple-element.17, s32[]{:T(128)S(6)} %select_n.62, ...), kind=kOutput, calls=%fused_computation.2 | convolution fusion | flops 2421424128 | bytes 15728644 | tf_op jit(solution)/shard_map/dot_general | solution.py:77
  202.1 0.7 fusion.1
  202.8 0.9 fusion.13
  203.8 0.8 copy.13
  204.7 0.7 fusion.12
  205.4 1.3 collective-permute-start.2
  206.7 19.7 %collective-permute-done.2 = bf16[128,3072]{1,0:T(8,128)(2,1)S(1)} collective-permute-done((bf16[128,3072]{1,0:T(8,128)(2,1)S(1)}, bf16[128,3072]{1,0:T(8,128)(2,1)S(1)}, u32[]{:S(2)}, u32[]{:S(2)}) %collective-permute-start.2) | collective-permute-done | bytes 786464 | tf_op jit(solution)/shard_map/ppermute | solution.py:18
  226.4 105.3 %all-gather.3.cloned.1.call-done = f32[128,3,3072]{2,1,0:T(4,128)} async-done(((f32[4,3,3072]{2,1,0:T(4,128)}), f32[128,3,3072]{2,1,0:T(4,128)}) %all-gather.3.cloned.1.call-update) | async-done | bytes 4718608 | tf_op jit(solution)/shard_map/all_gather | solution.py:102
  331.7 4.2 %reduce_sum.69 = f32[4,3,3072]{2,1,0:T(4,128)S(1)} reduce(f32[32,4,3,3072]{3,2,1,0:T(4,128)} %bitcast.62, f32[]{:T(128)} %constant.71.clone.1), dimensions={0}, to_apply=%region_6.7 | reduce | flops 1142784 | bytes 4866052 | tf_op jit(solution)/shard_map/reduce_sum | solution.py:101
  335.8 0.8 copy.14
  336.6 0.9 copy.17
  (36 shorter events, 2.5 us)
Async XLA Ops:
  14.2 14.7 %copy-start = (bf16[1,128,3072]{2,1,0:T(8,128)(2,1)S(1)}, bf16[1,128,3072]{2,1,0:T(8,128)(2,1)}, u32[]{:S(2)}) copy-start(bf16[1,128,3072]{2,1,0:T(8,128)(2,1)} %param.4) | copy-start | bytes 2359300
  14.2 173.2 %all-to-all-start = ((bf16[32,96,1536]{2,1,0:T(8,128)(2,1)}), bf16[32,96,1536]{2,1,0:T(8,128)(2,1)}, u32[]{:S(2)}, u32[]{:S(2)}) async-start(bf16[32,96,1536]{2,1,0:T(8,128)(2,1)} %bitcast.61), calls=%async_computation | async-start | bytes 18874368 | tf_op jit(solution)/shard_map/all_to_all | solution.py:67
  28.8 0.9 copy-start.8
  28.8 302.9 %all-gather.3.cloned.1.call-start = ((), (), s32[]{:S(2)}) async-start(), calls=%async_computation.1 | async-start | bytes 6488064 | tf_op jit(solution)/shard_map/all_gather | solution.py:102
  28.9 1.2 copy-start.1
  31.4 5.6 %collective-permute-start = (bf16[2,128,3072]{2,1,0:T(8,128)(2,1)}, bf16[2,128,3072]{2,1,0:T(8,128)(2,1)}, u32[]{:S(2)}, u32[]{:S(2)}) collective-permute-start(bf16[2,128,3072]{2,1,0:T(8,128)(2,1)} %pad_maximum_fusion.1), channel_id=1, source_target_pairs={{0,1},{1,0},{2,3},{3,2},{4,5},{5,4},{6,7},{7,6},{8,9},{9,8},{10,11... | collective-permute-start | bytes 4718600 | tf_op jit(solution)/shard_map/ppermute | solution.py:12
  38.6 1.2 copy-start.2
  38.7 1.7 copy-start.4
  40.3 1.2 copy-start.6
  187.4 9.5 %copy-start.5 = (bf16[2,128,3072]{2,1,0:T(8,128)(2,1)S(1)}, bf16[2,128,3072]{2,1,0:T(8,128)(2,1)}, u32[]{:S(2)}) copy-start(bf16[2,128,3072]{2,1,0:T(8,128)(2,1)} %copy-done.4) | copy-start | bytes 4718596
  187.4 9.5 %copy-start.7 = (bf16[1,256,3072]{2,1,0:T(8,128)(2,1)S(1)}, bf16[1,256,3072]{2,1,0:T(8,128)(2,1)}, u32[]{:S(2)}) copy-start(bf16[1,256,3072]{2,1,0:T(8,128)(2,1)} %copy-done.6) | copy-start | bytes 4718596
  192.9 3.9 %copy-start.3 = (bf16[2,128,3072]{2,1,0:T(8,128)(2,1)S(1)}, bf16[2,128,3072]{2,1,0:T(8,128)(2,1)}, u32[]{:S(2)}) copy-start(bf16[2,128,3072]{2,1,0:T(8,128)(2,1)} %copy-done.2) | copy-start | bytes 4718596
  193.1 9.7 %collective-permute-start.1 = (bf16[128,3072]{1,0:T(8,128)(2,1)S(1)}, bf16[128,3072]{1,0:T(8,128)(2,1)S(1)}, u32[]{:S(2)}, u32[]{:S(2)}) collective-permute-start(bf16[128,3072]{1,0:T(8,128)(2,1)S(1)} %select_convert_fusion), channel_id=1, source_target_pairs={{0,1},{1,0},{2,3},{3,2},{4,5},{5,4},{6,7},{7,6},{8,9},{9,8},{10,11... | collective-permute-start | bytes 2359304 | tf_op jit(solution)/shard_map/ppermute | solution.py:12
  205.4 21.0 %collective-permute-start.2 = (bf16[128,3072]{1,0:T(8,128)(2,1)S(1)}, bf16[128,3072]{1,0:T(8,128)(2,1)S(1)}, u32[]{:S(2)}, u32[]{:S(2)}) collective-permute-start(bf16[128,3072]{1,0:T(8,128)(2,1)S(1)} %fusion.12), channel_id=1, source_target_pairs={{32,0},{64,32},{96,64},{128,96},{160,128},{192,160},{224,192},{256... | collective-permute-start | bytes 2359304 | tf_op jit(solution)/shard_map/ppermute | solution.py:18
Sparse Core Ops, SparseCore 0:
  204.8 126.8 all-gather.2
